TPU v7x, 128 devices: a whole 4x4x4 slice. The times are simulated.
128 devices in a mesh: row: 8 (over x_hi, z), col: 8 (over x_lo, y), layer: 2 (over core).
Axes of the slice: x: 4 (x_hi: 2, x_lo: 2; x = x_hi * 2 + x_lo), y: 4, z: 4, core: 2. Of those that a mesh axis runs over, the one named last changes fastest.
Arguments:
- matrix: float32 [32, 512, 32, 512], P('row', None, 'col', 'layer'), may hold values from -40 to 40, as said below
- transforms: float32 [1, 16, 1024, 1024], P(None, 'row', ('col', 'layer')), may hold values from -0.1875 to 0.1875
Outputs:
- swept: float32 [32, 512, 32, 512], P('row', None, 'col', 'layer')
Inputs may be any that keep to these rules, and one draw needn't show every extreme that they name: `matrix`: symmetric: entry [i, a, j, b] equals entry [j, b, i, a].
All inputs are finite; a program needn't handle non-finite values.
Results may differ from a plain program's by a relative error of at most 0.0001.
Values sent between devices are 32-bit elements; how exact they have to be, the bound alone decides.
No kernel may reach another device: no remote copies, remote signals or barrier semaphores. Data moves between devices by JAX's collectives and lax.ppermute only.
A program may use at most 192 MiB of HBM per device.

v0:
```python
import jax
import jax.numpy as jnp
from jax import lax
from jax.sharding import PartitionSpec as P

exact_mode = lax.Precision.HIGHEST


def broadcast(x, axis, root):
    mine = lax.axis_index(axis) == root
    return lax.psum(jnp.where(mine, x, jnp.zeros_like(x)), axis)


def cut_along(x, dim, count):
    before, after = (x.shape[:dim], x.shape[dim + 1 :])
    return jnp.moveaxis(x.reshape(*before, count, -1, *after), dim, 0)


def sum_at_owner(x, axis, dim):
    count = lax.axis_size(axis)
    blocks = lax.all_to_all(cut_along(x, dim, count), axis, 0, 0, tiled=True)
    return jnp.sum(blocks, axis=0)


def passed_along(block, axis, distance):
    devices = range(lax.axis_size(axis))
    route = [(i - distance, i) for i in devices if i - distance in devices]
    return lax.ppermute(block, axis, route)


def split_slots(array, axis_dim):
    return [
        lax.index_in_dim(array, index, axis_dim, keepdims=False)
        for index in range(array.shape[axis_dim])
    ]


def leading(slots):
    width = len(slots)
    return slots[width - 2]


def rearranged(slots, from_prev, from_next, position, count):
    width = len(slots)
    result = [jnp.where(position == 0, slots[0], from_prev)]
    for local in range(1, width):
        if local % 2 == 1:
            if local == width - 1:
                result.append(jnp.where(position == count - 1, slots[width - 2], from_next))
            else:
                result.append(slots[local + 2])
        else:
            result.append(jnp.where(position == 0, slots[1], slots[0]))
    return result


def shards(matrix, transforms):
    pair_dev = matrix.shape[0] // 2
    block_size = matrix.shape[1]
    half_width = matrix.shape[3]
    width = 2 * pair_dev
    pairs_row = lax.axis_size("row")
    pairs_col = lax.axis_size("col")
    row_pos = lax.axis_index("row")
    col_pos = lax.axis_index("col")
    layer_pos = lax.axis_index("layer")
    current = matrix
    left_panel = lax.all_gather(transforms[0], ("col", "layer"), axis=1, tiled=True)
    shaped = left_panel.reshape(pair_dev, 2, block_size, 2 * block_size)
    selected = lax.dynamic_slice_in_dim(shaped, layer_pos * half_width, half_width, 2)
    right_part = broadcast(selected, "row", col_pos)
    grouped = current.reshape(pair_dev, 2 * block_size, width * half_width)
    partial_rows = jnp.einsum(
        "pka,pkc->pac",
        left_panel,
        grouped,
        precision=exact_mode,
        preferred_element_type=jnp.float32,
    )
    partial_rows = partial_rows.reshape(pair_dev, 2 * block_size, pair_dev, 2, half_width)
    term_pairs = jnp.einsum(
        "paqmh,qmhb->paqb",
        partial_rows,
        right_part,
        precision=exact_mode,
        preferred_element_type=jnp.float32,
    )
    term_pairs = term_pairs.reshape(pair_dev, 2 * block_size, pair_dev, 2, 2, half_width)
    rotated = sum_at_owner(term_pairs, "layer", 4)
    rotated = rotated.reshape(width, block_size, width, half_width)
    rows = split_slots(rotated, 0)
    upward = passed_along(leading(rows), "row", 1)
    downward = passed_along(rows[1], "row", -1)
    moved = jnp.stack(rearranged(rows, upward, downward, row_pos, pairs_row), 0)
    cols = split_slots(moved, 2)
    upward_cols = passed_along(leading(cols), "col", 1)
    downward_cols = passed_along(cols[1], "col", -1)
    current = jnp.stack(rearranged(cols, upward_cols, downward_cols, col_pos, pairs_col), 2)
    return current


def solution(mesh):
    return jax.shard_map(
        shards,
        mesh=mesh,
        in_specs=(P("row", None, "col", "layer"), P(None, "row", ("col", "layer"), None)),
        out_specs=P("row", None, "col", "layer"),
        check_vma=False,
    )
```

profile of v0, /device:TPU:120, one launch (start us, length us, event | category | flops | bytes accessed | tf_op | source)
XLA Modules:
  0.0 413.2 jit_solution(15162404626442989335)
XLA Ops:
  6.5 0.7 all-gather.3.cloned.1.call-update
  7.3 0.0 all-reduce.2.cloned.1.call-start
  7.3 54.8 %all-gather.3.cloned.1.call-done = f32[1,2,1024,1024]{3,2,1,0:T(8,128)} async-done(((f32[1,2,64,1024]{3,2,1,0:T(8,128)}), f32[1,2,1024,1024]{3,2,1,0:T(8,128)}) %all-gather.3.cloned.1.call-update) | async-done | bytes 8388624 | tf_op jit(solution)/shard_map/all_gather | solution.py:68
  62.1 4.8 %constant_dynamic-slice_fusion = f32[2,2,256,1024]{3,2,1,0:T(8,128)} fusion(f32[2,2,512,1024]{3,2,1,0:T(8,128)} %bitcast.73, s32[]{:T(128)S(6)} %select_n.56), kind=kLoop, calls=%fused_computation.23 | loop fusion | bytes 8388612 | tf_op jit(solution)/shard_map/dynamic_slice | solution.py:70
  66.9 5.4 %copy.45 = f32[2,2,256,1024]{2,3,1,0:T(8,128)} copy(f32[2,2,256,1024]{3,2,1,0:T(8,128)} %constant_dynamic-slice_fusion) | data formatting | bytes 8388608
  72.3 4.5 %broadcast_select_fusion = f32[2,2,256,1024]{2,3,1,0:T(8,128)} fusion(f32[2,2,256,1024]{2,3,1,0:T(8,128)} %copy.45, pred[]{:T(512)S(6)} %eq.19), kind=kLoop, calls=%fused_computation.20 | loop fusion | flops 1048576 | bytes 8388609 | tf_op jit(solution)/shard_map/jit(_where)/select_n | solution.py:11
  76.9 10.7 %reshape.15 = f32[2,1024,1024]{2,1,0:T(8,128)} reshape(f32[4,512,4,256]{3,2,1,0:T(4,128)} %param.2) | data formatting | bytes 16777216 | tf_op jit(solution)/shard_map/reshape | solution.py:72
  87.6 31.5 %fusion.2 = f32[2,1024,1024]{1,2,0:T(8,128)} fusion(f32[2,1024,1024]{2,1,0:T(8,128)} %reshape.15, f32[1,2,1024,1024]{3,2,1,0:T(8,128)} %all-gather.3.cloned.1.call-done), kind=kOutput, calls=%fused_computation.5 | convolution fusion | flops 25769803776 | bytes 25165824 | tf_op jit(solution)/shard_map/pka,pkc->pac/dot_general | solution.py:73
  119.1 66.1 %all-reduce.2.cloned.1.call-done = f32[2,2,256,1024]{2,3,1,0:T(8,128)} async-done(((f32[2,2,256,1024]{2,3,1,0:T(8,128)}), f32[2,2,256,1024]{2,3,1,0:T(8,128)}) %all-reduce.2.cloned.1.call-update) | async-done | bytes 4194320 | tf_op jit(solution)/shard_map/psum | solution.py:11
  185.2 31.1 %fusion = f32[2,1024,2,1024,1]{3,1,4,2,0:T(8,128)S(1)} fusion(f32[2,1024,2,2,256]{1,4,3,2,0:T(8,128)} %bitcast.72, f32[2,2,256,1024]{2,3,1,0:T(8,128)} %all-reduce.2.cloned.1.call-done), kind=kOutput, calls=%fused_computation.3 | convolution fusion | flops 25769803776 | bytes 29360128 | tf_op jit(solution)/shard_map/paqmh,qmhb->paqb/dot_general | solution.py:81
  216.3 2.9 copy.55
  219.2 19.0 %all_to_all.5 = f32[2,2,1024,2,2,1,256]{2,6,4,1,3,5,0:T(8,128)} all-to-all(f32[2,2,1024,2,2,1,256]{2,6,4,1,3,5,0:T(8,128)S(1)} %bitcast.68), channel_id=1, replica_groups=mesh['row'=8,'col'=8,'layer'=2] {'layer'}, dimensions={0} | all-to-all | bytes 33554432 | tf_op jit(solution)/shard_map/all_to_all | solution.py:21
  238.3 12.2 %reduce_sum.9 = f32[2,1024,2,2,256]{1,4,3,0,2:T(8,128)} reduce(f32[2,2,1024,2,2,1,256]{2,6,4,1,3,5,0:T(8,128)} %all_to_all.5, f32[]{:T(128)} %constant.21.clone.1), dimensions={0,5}, to_apply=%region_1.2 | reduce | flops 2097152 | bytes 25165828 | tf_op jit(solution)/shard_map/reduce_sum | solution.py:22
  250.5 8.7 %copy.29 = f32[2,1024,2,2,256]{4,1,0,3,2:T(8,128)} copy(f32[2,1024,2,2,256]{1,4,3,0,2:T(8,128)} %reduce_sum.9) | data formatting | bytes 16777216 | tf_op jit(solution)/shard_map/reduce_sum | solution.py:22
  259.2 5.4 %slice_bitcast_fusion.3 = (f32[512,4,256]{2,0,1:T(8,128)}, f32[512,4,256]{2,0,1:T(8,128)}, f32[1,512,4,256]{3,1,2,0:T(8,128)S(1)}) fusion(f32[4,512,4,256]{3,1,0,2:T(8,128)} %bitcast.69), kind=kLoop, calls=%fused_computation.11 | loop fusion | bytes 12582912 | tf_op jit(solution)/shard_map/squeeze | solution.py:33
  264.6 4.7 %collective-permute-start = (f32[512,4,256]{2,0,1:T(8,128)}, f32[512,4,256]{2,0,1:T(8,128)}, u32[]{:S(2)}, u32[]{:S(2)}) collective-permute-start(f32[512,4,256]{2,0,1:T(8,128)} %get-tuple-element.12), channel_id=1, source_target_pairs={{0,16},{16,32},{32,48},{48,64},{64,80},{80,96},{96,112},{1,17},{17... | collective-permute-start | bytes 6291464 | tf_op jit(solution)/shard_map/ppermute | solution.py:28
  269.3 1.9 collective-permute-start.1
  271.2 2.5 bitcast_select_fusion.3
  273.7 41.0 %collective-permute-done = f32[512,4,256]{2,0,1:T(8,128)} collective-permute-done((f32[512,4,256]{2,0,1:T(8,128)}, f32[512,4,256]{2,0,1:T(8,128)}, u32[]{:S(2)}, u32[]{:S(2)}) %collective-permute-start) | collective-permute-done | bytes 2097184 | tf_op jit(solution)/shard_map/ppermute | solution.py:28
  314.8 7.7 %collective-permute-done.1 = f32[512,4,256]{2,0,1:T(8,128)} collective-permute-done((f32[512,4,256]{2,0,1:T(8,128)}, f32[512,4,256]{2,0,1:T(8,128)}, u32[]{:S(2)}, u32[]{:S(2)}) %collective-permute-start.1) | collective-permute-done | bytes 2097184 | tf_op jit(solution)/shard_map/ppermute | solution.py:28
  322.5 4.2 %fusion.6 = (f32[1,512,4,256]{3,1,2,0:T(8,128)S(1)}, f32[1,512,4,256]{3,1,2,0:T(8,128)S(1)}) fusion(f32[512,4,256]{2,0,1:T(8,128)} %collective-permute-done, f32[4,512,4,256]{3,1,0,2:T(8,128)} %bitcast.71, pred[]{:T(512)S(6)} %eq.18, f32[512,4,256]{2,0,1:T(8,128)} %collective-permute-done.1, pred[]{:T(512)S(6)} %eq.20), kind=kLoop, calls=%fused_computation.16 | loop fusion | flops 1048576 | bytes 12582914 | tf_op jit(solution)/shard_map/stack | solution.py:94
  326.7 1.0 pad_maximum_fusion
  327.8 3.0 slice_bitcast_fusion.1
  330.8 1.6 copy-done
  332.4 3.3 collective-permute-start.2
  335.7 2.5 collective-permute-start.3
  338.3 2.5 bitcast_select_fusion.1
  340.8 40.3 %collective-permute-done.2 = f32[4,512,256]{2,1,0:T(8,128)} collective-permute-done((f32[4,512,256]{2,1,0:T(8,128)}, f32[4,512,256]{2,1,0:T(8,128)}, u32[]{:S(2)}, u32[]{:S(2)}) %collective-permute-start.2) | collective-permute-done | bytes 2097184 | tf_op jit(solution)/shard_map/ppermute | solution.py:28
  381.1 5.1 %collective-permute-done.3 = f32[4,512,256]{2,1,0:T(8,128)} collective-permute-done((f32[4,512,256]{2,1,0:T(8,128)}, f32[4,512,256]{2,1,0:T(8,128)}, u32[]{:S(2)}, u32[]{:S(2)}) %collective-permute-start.3) | collective-permute-done | bytes 2097184 | tf_op jit(solution)/shard_map/ppermute | solution.py:28
  386.3 4.2 %fusion.5 = (f32[4,512,1,256]{3,1,0,2:T(8,128)S(1)}, f32[4,512,1,256]{3,1,0,2:T(8,128)S(1)}) fusion(f32[4,512,256]{2,1,0:T(8,128)} %collective-permute-done.2, f32[4,512,4,256]{3,1,2,0:T(8,128)} %copy-done, pred[]{:T(512)S(6)} %eq.17, f32[4,512,256]{2,1,0:T(8,128)} %collective-permute-done.3, pred[]{:T(512)S(6)} %eq.21), kind=kLoop, calls=%fused_computation.13 | loop fusion | flops 1048576 | bytes 12582914 | tf_op jit(solution)/shard_map/stack | solution.py:98
  390.5 3.7 pad_maximum_fusion.1
  394.2 12.2 %copy.38 = f32[4,512,4,256]{3,2,1,0:T(4,128)} copy(f32[4,512,4,256]{3,1,0,2:T(8,128)} %pad_maximum_fusion.1) | data formatting | bytes 16777216 | tf_op jit(solution)/shard_map/stack | solution.py:98
  (3 shorter events, 0.0 us)
Async XLA Ops:
  6.5 55.6 %all-gather.3.cloned.1.call-start = ((), (), s32[]{:S(2)}) async-start(), calls=%async_computation.2 | async-start | bytes 8912896 | tf_op jit(solution)/shard_map/all_gather | solution.py:68
  7.3 177.9 %all-reduce.2.cloned.1.call-start = ((), (), s32[]{:S(2)}) async-start(), calls=%async_computation.1 | async-start | bytes 8388608 | tf_op jit(solution)/shard_map/psum | solution.py:11
  264.6 50.2 %collective-permute-start = (f32[512,4,256]{2,0,1:T(8,128)}, f32[512,4,256]{2,0,1:T(8,128)}, u32[]{:S(2)}, u32[]{:S(2)}) collective-permute-start(f32[512,4,256]{2,0,1:T(8,128)} %get-tuple-element.12), channel_id=1, source_target_pairs={{0,16},{16,32},{32,48},{48,64},{64,80},{80,96},{96,112},{1,17},{17... | collective-permute-start | bytes 6291464 | tf_op jit(solution)/shard_map/ppermute | solution.py:28
  269.3 53.2 %collective-permute-start.1 = (f32[512,4,256]{2,0,1:T(8,128)}, f32[512,4,256]{2,0,1:T(8,128)}, u32[]{:S(2)}, u32[]{:S(2)}) collective-permute-start(f32[512,4,256]{2,0,1:T(8,128)} %get-tuple-element.13), channel_id=1, source_target_pairs={{16,0},{32,16},{48,32},{64,48},{80,64},{96,80},{112,96},{17,1},{33... | collective-permute-start | bytes 6291464 | tf_op jit(solution)/shard_map/ppermute | solution.py:28
  327.7 4.7 %copy-start = (f32[4,512,4,256]{3,1,2,0:T(8,128)}, f32[4,512,4,256]{3,1,2,0:T(8,128)S(1)}, u32[]{:S(2)}) copy-start(f32[4,512,4,256]{3,1,2,0:T(8,128)S(1)} %pad_maximum_fusion) | copy-start | bytes 25165828
  332.4 48.7 %collective-permute-start.2 = (f32[4,512,256]{2,1,0:T(8,128)}, f32[4,512,256]{2,1,0:T(8,128)}, u32[]{:S(2)}, u32[]{:S(2)}) collective-permute-start(f32[4,512,256]{2,1,0:T(8,128)} %get-tuple-element.7), channel_id=1, source_target_pairs={{0,2},{2,4},{4,6},{6,8},{8,10},{10,12},{12,14},{1,3},{3,5},{5,7},{... | collective-permute-start | bytes 6291464 | tf_op jit(solution)/shard_map/ppermute | solution.py:28
  335.7 50.6 %collective-permute-start.3 = (f32[4,512,256]{2,1,0:T(8,128)}, f32[4,512,256]{2,1,0:T(8,128)}, u32[]{:S(2)}, u32[]{:S(2)}) collective-permute-start(f32[4,512,256]{2,1,0:T(8,128)} %get-tuple-element.8), channel_id=1, source_target_pairs={{2,0},{4,2},{6,4},{8,6},{10,8},{12,10},{14,12},{3,1},{5,3},{7,5},{... | collective-permute-start | bytes 6291464 | tf_op jit(solution)/shard_map/ppermute | solution.py:28
Sparse Core Ops, SparseCore 0:
  9.0 53.0 all-gather.2
  77.0 108.1 all-reduce.1
where the time goes:
time: 414 us; the launch traced here: 413 us
  waiting for transfers between devices  216 us (52%)
  matrix products  62.6 us (15%)
  local copies, waits for them, and re-layouts  54.7 us (13%)
  other arithmetic  34.9 us (8%)
  blocking collectives  19 us (5%)
  between operations  13.5 us (3%)
  starting transfers between devices  12.5 us (3%)
    ppermute x4, waiting for transfers between devices, passed_along(): return lax.ppermute(block, axis, route)  94.2 us
    psum x1, waiting for transfers between devices, broadcast(): return lax.psum(jnp.where(mine, x, jnp.zeros_like(x)), axis)  66.1 us
    all_gather x1, waiting for transfers between devices, shards(): lax.all_gather(transforms[0], ('col', 'layer'), axis=1, tiled=True)  54.8 us
    dot_general x1, matrix products, shards(): jnp.einsum('pka,pkc->pac', left_panel, grouped, precision=exact_mode, pre...  31.5 us
    dot_general x1, matrix products, shards(): jnp.einsum('paqmh,qmhb->paqb', partial_rows, right_part, precision=exact_...  31.1 us
    all_to_all x1, blocking collectives, sum_at_owner(): blocks = lax.all_to_all(cut_along(x, dim, count), axis, 0, 0, tiled=True)  19 us
    ppermute x4, starting transfers between devices, passed_along(): return lax.ppermute(block, axis, route)  12.5 us
    reduce_sum x1, other arithmetic, sum_at_owner(): return jnp.sum(blocks, axis=0)  12.2 us
  transfers between devices with their start and end apart: 6, of which 6 were waited for; matrix products, arithmetic and copies ran while one was open for 11% of the time, Pallas kernels for 0%

commit v1 on v0

--- a/solution.py
+++ b/solution.py
@@ -65,7 +65,16 @@
     col_pos = lax.axis_index("col")
     layer_pos = lax.axis_index("layer")
     current = matrix
-    left_panel = lax.all_gather(transforms[0], ("col", "layer"), axis=1, tiled=True)
+    z_in = transforms[0]
+    left_panel = jnp.concatenate(
+        lax.all_to_all(
+            jnp.stack(tuple((z_in for _ in range(lax.axis_size(("col", "layer")))))),
+            ("col", "layer"),
+            0,
+            0,
+        ),
+        axis=1,
+    )
     shaped = left_panel.reshape(pair_dev, 2, block_size, 2 * block_size)
     selected = lax.dynamic_slice_in_dim(shaped, layer_pos * half_width, half_width, 2)
     right_part = broadcast(selected, "row", col_pos)

time: 414 us -> 503 us (1.21)
  waiting for transfers between devices: 216 us -> 288 us
  local copies, waits for them, and re-layouts: 54.7 us -> 65.3 us
  starting transfers between devices: 12.5 us -> 18.1 us
    all_to_all x0 -> x1, waiting for transfers between devices: none -> 128 us  [shards(): lax.all_to_all(jnp.stack(tuple((z_in for _ in range(lax.axis_size(('col',...]
    all_gather x1 -> x0, waiting for transfers between devices: 54.8 us -> none  [shards(): lax.all_gather(transforms[0], ('col', 'layer'), axis=1, tiled=True)]
    all_to_all x0 -> x1, starting transfers between devices: none -> 5.63 us  [shards(): lax.all_to_all(jnp.stack(tuple((z_in for _ in range(lax.axis_size(('col',...]
    another operation x0 -> x1, local copies, waits for them, and re-layouts: none -> 5.5 us  [shards(): jnp.stack(tuple((z_in for _ in range(lax.axis_size(('col', 'layer'))))))]
    unnamed x3 -> x5, local copies, waits for them, and re-layouts: 6.99 us -> 10.4 us
  transfers between devices with their start and end apart: 6 -> 6, of which waited for: 6 -> 6; matrix products, arithmetic and copies ran while one was open for 11% -> 9% of each run, Pallas kernels for 0% -> 0%
where the time goes in v1:
time: 503 us; the launch traced here: 502 us
  waiting for transfers between devices  288 us (57%)
  local copies, waits for them, and re-layouts  65.3 us (13%)
  matrix products  62.6 us (12%)
  other arithmetic  34.9 us (7%)
  blocking collectives  19 us (4%)
  starting transfers between devices  18.1 us (4%)
  between operations  13.5 us (3%)
    all_to_all x1, waiting for transfers between devices, shards(): lax.all_to_all(jnp.stack(tuple((z_in for _ in range(lax.axis_size(('col',...  128 us
    ppermute x4, waiting for transfers between devices, passed_along(): return lax.ppermute(block, axis, route)  94.2 us
    psum x1, waiting for transfers between devices, broadcast(): return lax.psum(jnp.where(mine, x, jnp.zeros_like(x)), axis)  65.7 us
    dot_general x1, matrix products, shards(): jnp.einsum('pka,pkc->pac', left_panel, grouped, precision=exact_mode, pre...  31.5 us
    dot_general x1, matrix products, shards(): jnp.einsum('paqmh,qmhb->paqb', partial_rows, right_part, precision=exact_...  31.1 us
    all_to_all x1, blocking collectives, sum_at_owner(): blocks = lax.all_to_all(cut_along(x, dim, count), axis, 0, 0, tiled=True)  19 us
    ppermute x4, starting transfers between devices, passed_along(): return lax.ppermute(block, axis, route)  12.5 us
    reduce_sum x1, other arithmetic, sum_at_owner(): return jnp.sum(blocks, axis=0)  12.2 us
  transfers between devices with their start and end apart: 6, of which 6 were waited for; matrix products, arithmetic and copies ran while one was open for 9% of the time, Pallas kernels for 0%

profile of v1, /device:TPU:120, one launch (start us, length us, event | category | flops | bytes accessed | tf_op | source)
XLA Modules:
  0.0 501.7 jit_solution(2771019786056694332)
XLA Ops:
  6.5 5.5 %stack.23 = f32[16,2,64,1024]{3,2,1,0:T(8,128)} broadcast(f32[2,64,1024]{2,1,0:T(8,128)} %bitcast.78), dimensions={1,2,3} | broadcast | bytes 8912896 | tf_op jit(solution)/shard_map/stack | solution.py:71
  12.0 5.6 %all-to-all-start = ((f32[16,2,64,1024]{3,2,1,0:T(8,128)}), f32[16,2,64,1024]{3,2,1,0:T(8,128)}, u32[]{:S(2)}, u32[]{:S(2)}) async-start(f32[16,2,64,1024]{3,2,1,0:T(8,128)} %stack.23), calls=%async_computation | async-start | bytes 16777216 | tf_op jit(solution)/shard_map/all_to_all | solution.py:70
  17.7 128.2 %all-to-all-done = f32[16,2,64,1024]{3,2,1,0:T(8,128)} async-done(((f32[16,2,64,1024]{3,2,1,0:T(8,128)}), f32[16,2,64,1024]{3,2,1,0:T(8,128)}, u32[]{:S(2)}, u32[]{:S(2)}) %all-to-all-start) | async-done | bytes 8388640 | tf_op jit(solution)/shard_map/all_to_all | solution.py:70
  145.9 4.2 copy.23
  150.2 3.4 copy-done.1
  153.6 2.3 constant_dynamic-slice_fusion
  155.8 5.4 %copy.45 = f32[2,2,256,1024]{2,3,1,0:T(8,128)} copy(f32[2,2,256,1024]{3,2,1,0:T(8,128)} %constant_dynamic-slice_fusion) | data formatting | bytes 8388608
  161.2 4.5 broadcast_select_fusion
  165.8 10.7 %reshape.20 = f32[2,1024,1024]{2,1,0:T(8,128)} reshape(f32[4,512,4,256]{3,2,1,0:T(4,128)} %param.2) | data formatting | bytes 16777216 | tf_op jit(solution)/shard_map/reshape | solution.py:81
  176.5 31.5 %fusion.5 = f32[2,1024,1024]{1,2,0:T(8,128)} fusion(f32[2,1024,1024]{2,1,0:T(8,128)} %bitcast.76, f32[2,1024,1024]{2,1,0:T(8,128)} %reshape.20), kind=kOutput, calls=%fused_computation.22 | convolution fusion | flops 25769803776 | bytes 25165824 | tf_op jit(solution)/shard_map/pka,pkc->pac/dot_general | solution.py:82
  208.0 65.7 %all-reduce.2.cloned.1.call-done = f32[2,2,256,1024]{2,3,1,0:T(8,128)} async-done(((f32[2,2,256,1024]{2,3,1,0:T(8,128)}), f32[2,2,256,1024]{2,3,1,0:T(8,128)}) %all-reduce.2.cloned.1.call-update) | async-done | bytes 4194320 | tf_op jit(solution)/shard_map/psum | solution.py:11
  273.7 31.1 %fusion = f32[2,1024,2,1024,1]{3,1,4,2,0:T(8,128)S(1)} fusion(f32[2,1024,2,2,256]{1,4,3,2,0:T(8,128)} %bitcast.77, f32[2,2,256,1024]{2,3,1,0:T(8,128)} %all-reduce.2.cloned.1.call-done), kind=kOutput, calls=%fused_computation.3 | convolution fusion | flops 25769803776 | bytes 29360128 | tf_op jit(solution)/shard_map/paqmh,qmhb->paqb/dot_general | solution.py:90
  304.8 2.9 copy.55
  307.7 19.0 %all_to_all.10 = f32[2,2,1024,2,2,1,256]{2,6,4,1,3,5,0:T(8,128)} all-to-all(f32[2,2,1024,2,2,1,256]{2,6,4,1,3,5,0:T(8,128)S(1)} %bitcast.71), channel_id=1, replica_groups=mesh['row'=8,'col'=8,'layer'=2] {'layer'}, dimensions={0} | all-to-all | bytes 33554432 | tf_op jit(solution)/shard_map/all_to_all | solution.py:21
  326.8 12.2 %reduce_sum.9 = f32[2,1024,2,2,256]{1,4,3,0,2:T(8,128)} reduce(f32[2,2,1024,2,2,1,256]{2,6,4,1,3,5,0:T(8,128)} %all_to_all.10, f32[]{:T(128)} %constant.21.clone.1), dimensions={0,5}, to_apply=%region_1.2 | reduce | flops 2097152 | bytes 25165828 | tf_op jit(solution)/shard_map/reduce_sum | solution.py:22
  339.0 8.7 %copy.29 = f32[2,1024,2,2,256]{4,1,0,3,2:T(8,128)} copy(f32[2,1024,2,2,256]{1,4,3,0,2:T(8,128)} %reduce_sum.9) | data formatting | bytes 16777216 | tf_op jit(solution)/shard_map/reduce_sum | solution.py:22
  347.7 5.4 %slice_bitcast_fusion.3 = (f32[512,4,256]{2,0,1:T(8,128)}, f32[512,4,256]{2,0,1:T(8,128)}, f32[1,512,4,256]{3,1,2,0:T(8,128)S(1)}) fusion(f32[4,512,4,256]{3,1,0,2:T(8,128)} %bitcast.72), kind=kLoop, calls=%fused_computation.9 | loop fusion | bytes 12582912 | tf_op jit(solution)/shard_map/squeeze | solution.py:33
  353.1 4.7 collective-permute-start
  357.8 1.9 collective-permute-start.1
  359.7 2.5 bitcast_select_fusion.3
  362.3 41.0 %collective-permute-done = f32[512,4,256]{2,0,1:T(8,128)} collective-permute-done((f32[512,4,256]{2,0,1:T(8,128)}, f32[512,4,256]{2,0,1:T(8,128)}, u32[]{:S(2)}, u32[]{:S(2)}) %collective-permute-start) | collective-permute-done | bytes 2097184 | tf_op jit(solution)/shard_map/ppermute | solution.py:28
  403.3 7.7 %collective-permute-done.1 = f32[512,4,256]{2,0,1:T(8,128)} collective-permute-done((f32[512,4,256]{2,0,1:T(8,128)}, f32[512,4,256]{2,0,1:T(8,128)}, u32[]{:S(2)}, u32[]{:S(2)}) %collective-permute-start.1) | collective-permute-done | bytes 2097184 | tf_op jit(solution)/shard_map/ppermute | solution.py:28
  411.0 4.2 fusion.4
  416.3 3.0 slice_bitcast_fusion.1
  420.9 3.3 collective-permute-start.2
  424.2 2.5 collective-permute-start.3
  426.8 2.5 bitcast_select_fusion.1
  429.3 40.3 %collective-permute-done.2 = f32[4,512,256]{2,1,0:T(8,128)} collective-permute-done((f32[4,512,256]{2,1,0:T(8,128)}, f32[4,512,256]{2,1,0:T(8,128)}, u32[]{:S(2)}, u32[]{:S(2)}) %collective-permute-start.2) | collective-permute-done | bytes 2097184 | tf_op jit(solution)/shard_map/ppermute | solution.py:28
  469.6 5.1 %collective-permute-done.3 = f32[4,512,256]{2,1,0:T(8,128)} collective-permute-done((f32[4,512,256]{2,1,0:T(8,128)}, f32[4,512,256]{2,1,0:T(8,128)}, u32[]{:S(2)}, u32[]{:S(2)}) %collective-permute-start.3) | collective-permute-done | bytes 2097184 | tf_op jit(solution)/shard_map/ppermute | solution.py:28
  474.8 4.2 fusion.3
  479.0 3.7 pad_maximum_fusion.1
  482.7 12.2 %copy.38 = f32[4,512,4,256]{3,2,1,0:T(4,128)} copy(f32[4,512,4,256]{3,1,0,2:T(8,128)} %pad_maximum_fusion.1) | data formatting | bytes 16777216 | tf_op jit(solution)/shard_map/stack | solution.py:107
  (6 shorter events, 2.7 us)
Async XLA Ops:
  12.0 133.9 %all-to-all-start = ((f32[16,2,64,1024]{3,2,1,0:T(8,128)}), f32[16,2,64,1024]{3,2,1,0:T(8,128)}, u32[]{:S(2)}, u32[]{:S(2)}) async-start(f32[16,2,64,1024]{3,2,1,0:T(8,128)} %stack.23), calls=%async_computation | async-start | bytes 16777216 | tf_op jit(solution)/shard_map/all_to_all | solution.py:70
  17.7 256.0 %all-reduce.2.cloned.1.call-start = ((), (), s32[]{:S(2)}) async-start(), calls=%async_computation.2 | async-start | bytes 8388608 | tf_op jit(solution)/shard_map/psum | solution.py:11
  150.2 3.4 copy-start.1
  353.1 50.2 %collective-permute-start = (f32[512,4,256]{2,0,1:T(8,128)}, f32[512,4,256]{2,0,1:T(8,128)}, u32[]{:S(2)}, u32[]{:S(2)}) collective-permute-start(f32[512,4,256]{2,0,1:T(8,128)} %get-tuple-element.12), channel_id=1, source_target_pairs={{0,16},{16,32},{32,48},{48,64},{64,80},{80,96},{96,112},{1,17},{17... | collective-permute-start | bytes 6291464 | tf_op jit(solution)/shard_map/ppermute | solution.py:28
  357.8 53.2 %collective-permute-start.1 = (f32[512,4,256]{2,0,1:T(8,128)}, f32[512,4,256]{2,0,1:T(8,128)}, u32[]{:S(2)}, u32[]{:S(2)}) collective-permute-start(f32[512,4,256]{2,0,1:T(8,128)} %get-tuple-element.13), channel_id=1, source_target_pairs={{16,0},{32,16},{48,32},{64,48},{80,64},{96,80},{112,96},{17,1},{33... | collective-permute-start | bytes 6291464 | tf_op jit(solution)/shard_map/ppermute | solution.py:28
  416.3 4.7 copy-start
  420.9 48.7 %collective-permute-start.2 = (f32[4,512,256]{2,1,0:T(8,128)}, f32[4,512,256]{2,1,0:T(8,128)}, u32[]{:S(2)}, u32[]{:S(2)}) collective-permute-start(f32[4,512,256]{2,1,0:T(8,128)} %get-tuple-element.7), channel_id=1, source_target_pairs={{0,2},{2,4},{4,6},{6,8},{8,10},{10,12},{12,14},{1,3},{3,5},{5,7},{... | collective-permute-start | bytes 6291464 | tf_op jit(solution)/shard_map/ppermute | solution.py:28
  424.2 50.6 %collective-permute-start.3 = (f32[4,512,256]{2,1,0:T(8,128)}, f32[4,512,256]{2,1,0:T(8,128)}, u32[]{:S(2)}, u32[]{:S(2)}) collective-permute-start(f32[4,512,256]{2,1,0:T(8,128)} %get-tuple-element.8), channel_id=1, source_target_pairs={{2,0},{4,2},{6,4},{8,6},{10,8},{12,10},{14,12},{3,1},{5,3},{7,5},{... | collective-permute-start | bytes 6291464 | tf_op jit(solution)/shard_map/ppermute | solution.py:28
Sparse Core Ops, SparseCore 0:
  165.9 107.7 all-reduce.1
